TPU v7x, 32 devices: a whole 2x2x4 slice. The times are simulated.
32 devices in a mesh: dp: 16 (over z, y, x), tensor: 2 (over core).
Axes of the slice: x: 2, y: 2, z: 4, core: 2. Of those that a mesh axis runs over, the one named last changes fastest.
Arguments:
- inputs: bfloat16 [17664, 1024], P(('dp', 'tensor')), may hold values from -6 to 6
- cotangent: bfloat16 [17664, 1024], P(('dp', 'tensor')), may hold values from -6 to 6
- slot_live: int32 [16], P('dp'), may hold values from 0 to 1, as said below
- token_type: int32 [17664], P(('dp', 'tensor')), may hold values from 0 to 3, as said below
- attn_norm_gain: bfloat16 [1024], P('dp'), may hold values from 0.25 to 1.75
- attn_norm_bias: bfloat16 [1024], P('dp'), may hold values from -4 to 4
- qkv_weight: bfloat16 [3, 1024, 1024], P(None, 'dp', 'tensor'), may hold values from -0.1875 to 0.1875
- proj_weight: bfloat16 [1024, 1024], P('tensor', 'dp'), may hold values from -1 to 1
- proj_bias: bfloat16 [1024], P('dp'), may hold values from -4 to 4
- mlp_norm_gain: bfloat16 [1024], P('dp'), may hold values from 0.25 to 1.75
- mlp_norm_bias: bfloat16 [1024], P('dp'), may hold values from -4 to 4
- fc1_weight: bfloat16 [1024, 4096], P('dp', 'tensor'), may hold values from -0.1875 to 0.1875
- fc1_bias: bfloat16 [4096], P(('tensor', 'dp')), may hold values from -6 to 6
- fc2_weight: bfloat16 [4096, 1024], P('tensor', 'dp'), may hold values from -0.09375 to 0.09375
- fc2_bias: bfloat16 [1024], P('dp'), may hold values from -4 to 4
Outputs:
- outputs: bfloat16 [17664, 1024], P(('dp', 'tensor'))
- grad_inputs: bfloat16 [17664, 1024], P(('dp', 'tensor'))
- grad_attn_norm_gain: float32 [1024], P('dp')
- grad_attn_norm_bias: float32 [1024], P('dp')
- grad_qkv_weight: float32 [3, 1024, 1024], P(None, 'dp', 'tensor')
- grad_proj_weight: float32 [1024, 1024], P('tensor', 'dp')
- grad_proj_bias: float32 [1024], P('dp')
- grad_mlp_norm_gain: float32 [1024], P('dp')
- grad_mlp_norm_bias: float32 [1024], P('dp')
- grad_fc1_weight: float32 [1024, 4096], P('dp', 'tensor')
- grad_fc1_bias: float32 [4096], P(('tensor', 'dp'))
- grad_fc2_weight: float32 [4096, 1024], P('tensor', 'dp')
- grad_fc2_bias: float32 [1024], P('dp')
Inputs may be any that keep to these rules, and one draw needn't show every extreme that they name: `slot_live`: the ones of each data group's 1 entries come first; some data group holds 1 sequence. `token_type`: in each sequence position 0 is 0; positions 1 to 77 are 1 up to a caption length of at least one and 3 after it; later positions are 2, except the last two, which are 3.
All inputs are finite; a program needn't handle non-finite values.
Results may differ from a plain program's by a relative error of at most 0.02.
Values may be sent and summed in bfloat16 or wider, within the bound.
No kernel may reach another device: no remote copies, remote signals or barrier semaphores. Data moves between devices by JAX's collectives and lax.ppermute only.
A program may use at most 256 MiB of HBM per device.

v0:
```python
import jax
import jax.numpy as jnp
from jax import lax
from jax.sharding import PartitionSpec as P

HEAD_DIM = 64
SEQ_LEN = 1104


def layer_norm(values, norm_gain, norm_shift):
    row_mean = jnp.mean(values, axis=-1, keepdims=True)
    centered = values - row_mean
    variance = jnp.mean(centered * centered, axis=-1, keepdims=True)
    return centered * lax.rsqrt(variance + 1e-05) * norm_gain + norm_shift


def exact_gelu(values):
    return jax.nn.gelu(values, approximate=False)


def masked_scores(query, keys, key_valid, score_scale):
    scores = (
        jnp.einsum("qhd,khd->hqk", query, keys, preferred_element_type=jnp.float32) * score_scale
    )
    return jnp.where(key_valid[None, None, :] > 0, scores, -1e30)


def attend_forward(query, keys, values, key_valid, score_scale):
    scores = masked_scores(query, keys, key_valid, score_scale)
    row_max = jnp.max(scores, axis=-1, keepdims=True)
    exp_scores = jnp.exp(scores - row_max)
    row_sum = jnp.sum(exp_scores, axis=-1, keepdims=True)
    attn_prob = (exp_scores / row_sum).astype(jnp.bfloat16)
    mixed = jnp.einsum("hqk,khd->qhd", attn_prob, values, preferred_element_type=jnp.float32)
    return (mixed.astype(jnp.bfloat16), row_max + jnp.log(row_sum))


def attend_backward(query, keys, values, key_valid, log_total, grad_mixed, score_scale):
    scores = masked_scores(query, keys, key_valid, score_scale)
    attn_prob = jnp.exp(scores - log_total)
    grad_prob = jnp.einsum("qhd,khd->hqk", grad_mixed, values, preferred_element_type=jnp.float32)
    row_dot = jnp.sum(attn_prob * grad_prob, axis=-1, keepdims=True)
    grad_scores = (attn_prob * (grad_prob - row_dot)).astype(jnp.bfloat16)
    grad_query = (
        jnp.einsum("hqk,khd->qhd", grad_scores, keys, preferred_element_type=jnp.float32)
        * score_scale
    )
    grad_keys = (
        jnp.einsum("hqk,qhd->khd", grad_scores, query, preferred_element_type=jnp.float32)
        * score_scale
    )
    grad_values = jnp.einsum(
        "hqk,qhd->khd",
        attn_prob.astype(jnp.bfloat16),
        grad_mixed,
        preferred_element_type=jnp.float32,
    )
    return (
        grad_query.astype(jnp.bfloat16),
        grad_keys.astype(jnp.bfloat16),
        grad_values.astype(jnp.bfloat16),
    )


def contract_rows(left, right):
    return lax.dot_general(
        left, right, (((0,), (0,)), ((), ())), preferred_element_type=jnp.float32
    )


def contract_cols(left, right):
    return lax.dot_general(
        left, right, (((1,), (1,)), ((), ())), preferred_element_type=jnp.float32
    )


def on_device(
    inputs,
    cotangent,
    slot_live,
    token_type,
    attn_norm_gain,
    attn_norm_bias,
    qkv_weight,
    proj_weight,
    proj_bias,
    mlp_norm_gain,
    mlp_norm_bias,
    fc1_weight,
    fc1_bias,
    fc2_weight,
    fc2_bias,
):
    tensor_size = lax.axis_size("tensor")
    tensor_rank = lax.axis_index("tensor")
    local_rows = inputs.shape[0]
    slot_count = slot_live.shape[0]
    whole_rows = local_rows * tensor_size
    width_here = qkv_weight.shape[2]
    heads_here = width_here // HEAD_DIM
    score_scale = HEAD_DIM ** (-0.5)
    position = tensor_rank * local_rows + jnp.arange(local_rows, dtype=jnp.int32)
    slot_of_row = position // SEQ_LEN
    slot_match = slot_of_row[:, None] == jnp.arange(slot_count, dtype=jnp.int32)[None, :]
    live_rows = jnp.sum(jnp.where(slot_match, slot_live.astype(jnp.float32)[None, :], 0.0), axis=1)
    live_col = live_rows[:, None]
    valid_local = (token_type != 3).astype(jnp.bfloat16)
    (
        qkv_full,
        proj_full,
        proj_bias_full,
        gain_one,
        shift_one,
        fc1_full,
        fc1_bias_full,
        fc2_full,
        gain_two,
        shift_two,
        fc2_bias_full,
    ) = (
        lax.all_gather(qkv_weight, "dp", axis=1, tiled=True),
        lax.all_gather(proj_weight, "dp", axis=1, tiled=True),
        lax.all_gather(proj_bias, "dp", axis=0, tiled=True),
        lax.all_gather(attn_norm_gain, "dp", axis=0, tiled=True),
        lax.all_gather(attn_norm_bias, "dp", axis=0, tiled=True),
        lax.all_gather(fc1_weight, "dp", axis=0, tiled=True),
        lax.all_gather(fc1_bias, "dp", axis=0, tiled=True),
        lax.all_gather(fc2_weight, "dp", axis=1, tiled=True),
        lax.all_gather(mlp_norm_gain, "dp", axis=0, tiled=True),
        lax.all_gather(mlp_norm_bias, "dp", axis=0, tiled=True),
        lax.all_gather(fc2_bias, "dp", axis=0, tiled=True),
    )
    gain_one_f = gain_one.astype(jnp.float32)
    shift_one_f = shift_one.astype(jnp.float32)
    rows_in = inputs.astype(jnp.float32)
    norm_one = layer_norm(rows_in, gain_one_f, shift_one_f).astype(jnp.bfloat16)
    whole_one, whole_valid = (
        lax.all_gather(norm_one, "tensor", axis=0, tiled=True),
        lax.all_gather(valid_local, "tensor", axis=0, tiled=True),
    )
    packed = jnp.einsum("nd,jdc->jnc", whole_one, qkv_full, preferred_element_type=jnp.float32)
    packed = packed.astype(jnp.bfloat16).reshape(3, slot_count, SEQ_LEN, heads_here, HEAD_DIM)
    valid_seq = whole_valid.reshape(slot_count, SEQ_LEN)

    def forward_slot(slot_index):
        slot_qkv = lax.dynamic_index_in_dim(packed, slot_index, 1, keepdims=False)
        slot_valid = lax.dynamic_index_in_dim(valid_seq, slot_index, 0, keepdims=False)
        return attend_forward(slot_qkv[0], slot_qkv[1], slot_qkv[2], slot_valid, score_scale)

    heads_out, log_total = lax.map(forward_slot, jnp.arange(slot_count, dtype=jnp.int32))
    mixed_flat = heads_out.reshape(whole_rows, width_here)
    row_block = mixed_flat
    attn_out = lax.psum_scatter(
        jnp.dot(row_block, proj_full, preferred_element_type=jnp.float32).astype(jnp.bfloat16),
        "tensor",
        scatter_dimension=0,
        tiled=True,
    ).astype(jnp.float32)
    middle = rows_in + live_col * (attn_out + proj_bias_full.astype(jnp.float32))
    gain_two_f = gain_two.astype(jnp.float32)
    shift_two_f = shift_two.astype(jnp.float32)
    fc1_bias_f = fc1_bias_full.astype(jnp.float32)
    norm_two = layer_norm(middle, gain_two_f, shift_two_f).astype(jnp.bfloat16)
    whole_two = lax.all_gather(norm_two, "tensor", axis=0, tiled=True)
    hidden_pre = jnp.dot(whole_two, fc1_full, preferred_element_type=jnp.float32) + fc1_bias_f
    hidden_act = exact_gelu(hidden_pre).astype(jnp.bfloat16)
    row_block = hidden_act
    mlp_out = lax.psum_scatter(
        jnp.dot(row_block, fc2_full, preferred_element_type=jnp.float32).astype(jnp.bfloat16),
        "tensor",
        scatter_dimension=0,
        tiled=True,
    ).astype(jnp.float32)
    result = middle + live_col * (mlp_out + fc2_bias_full.astype(jnp.float32))
    outputs = result.astype(jnp.bfloat16)
    grad_out = cotangent.astype(jnp.float32)
    grad_mlp = (live_col * grad_out).astype(jnp.bfloat16)
    grad_fc2_bias = jnp.sum(grad_mlp, axis=0, dtype=jnp.float32)
    whole_grad_mlp = lax.all_gather(grad_mlp, "tensor", axis=0, tiled=True)
    whole_two = lax.all_gather(norm_two, "tensor", axis=0, tiled=True)
    hidden_pre = jnp.dot(whole_two, fc1_full, preferred_element_type=jnp.float32) + fc1_bias_f
    hidden_act = exact_gelu(hidden_pre).astype(jnp.bfloat16)
    grad_fc2 = contract_rows(hidden_act, whole_grad_mlp)
    grad_act = contract_cols(whole_grad_mlp, fc2_full)
    unused, gelu_pull = jax.vjp(exact_gelu, hidden_pre)
    grad_pre = gelu_pull(grad_act)[0].astype(jnp.bfloat16)
    grad_fc1_bias = jnp.sum(grad_pre, axis=0, dtype=jnp.float32)
    grad_fc1 = contract_rows(whole_two, grad_pre)
    row_block = grad_pre
    grad_two = lax.psum_scatter(
        contract_cols(row_block, fc1_full).astype(jnp.bfloat16),
        "tensor",
        scatter_dimension=0,
        tiled=True,
    ).astype(jnp.float32)
    unused, norm_pull_two = jax.vjp(layer_norm, middle, gain_two_f, shift_two_f)
    grad_mid_norm, grad_gain_two, grad_shift_two = norm_pull_two(grad_two)
    grad_middle = grad_out + grad_mid_norm
    grad_branch = (live_col * grad_middle).astype(jnp.bfloat16)
    grad_proj_bias = jnp.sum(grad_branch, axis=0, dtype=jnp.float32)
    whole_grad_branch = lax.all_gather(grad_branch, "tensor", axis=0, tiled=True)
    grad_proj = contract_rows(mixed_flat, whole_grad_branch)
    grad_mixed = contract_cols(whole_grad_branch, proj_full).astype(jnp.bfloat16)
    grad_mixed_seq = grad_mixed.reshape(slot_count, SEQ_LEN, heads_here, HEAD_DIM)

    def backward_slot(slot_index):
        slot_qkv = lax.dynamic_index_in_dim(packed, slot_index, 1, keepdims=False)
        slot_valid = lax.dynamic_index_in_dim(valid_seq, slot_index, 0, keepdims=False)
        slot_total = lax.dynamic_index_in_dim(log_total, slot_index, 0, keepdims=False)
        slot_grad = lax.dynamic_index_in_dim(grad_mixed_seq, slot_index, 0, keepdims=False)
        return attend_backward(
            slot_qkv[0], slot_qkv[1], slot_qkv[2], slot_valid, slot_total, slot_grad, score_scale
        )

    grad_query, grad_keys, grad_values = lax.map(
        backward_slot, jnp.arange(slot_count, dtype=jnp.int32)
    )
    grad_packed = jnp.stack((grad_query, grad_keys, grad_values)).reshape(3, whole_rows, width_here)
    whole_one = lax.all_gather(norm_one, "tensor", axis=0, tiled=True)
    grad_qkv = jnp.einsum("nd,jnc->jdc", whole_one, grad_packed, preferred_element_type=jnp.float32)
    row_block = grad_packed
    grad_one = lax.psum_scatter(
        jnp.einsum("jnc,jdc->nd", row_block, qkv_full, preferred_element_type=jnp.float32).astype(
            jnp.bfloat16
        ),
        "tensor",
        scatter_dimension=0,
        tiled=True,
    ).astype(jnp.float32)
    unused, norm_pull_one = jax.vjp(layer_norm, rows_in, gain_one_f, shift_one_f)
    grad_in_norm, grad_gain_one, grad_shift_one = norm_pull_one(grad_one)
    grad_inputs = (grad_middle + grad_in_norm).astype(jnp.bfloat16)
    (
        out_qkv,
        out_proj,
        sum_proj_bias,
        sum_gain_one,
        sum_shift_one,
        out_fc1,
        out_fc1_bias,
        out_fc2,
        sum_gain_two,
        sum_shift_two,
        sum_fc2_bias,
    ) = (
        lax.psum_scatter(
            grad_qkv.astype(jnp.bfloat16), "dp", scatter_dimension=1, tiled=True
        ).astype(jnp.float32),
        lax.psum_scatter(
            grad_proj.astype(jnp.bfloat16), "dp", scatter_dimension=1, tiled=True
        ).astype(jnp.float32),
        lax.psum_scatter(
            grad_proj_bias.astype(jnp.bfloat16), "dp", scatter_dimension=0, tiled=True
        ).astype(jnp.float32),
        lax.psum_scatter(
            grad_gain_one.astype(jnp.bfloat16), "dp", scatter_dimension=0, tiled=True
        ).astype(jnp.float32),
        lax.psum_scatter(
            grad_shift_one.astype(jnp.bfloat16), "dp", scatter_dimension=0, tiled=True
        ).astype(jnp.float32),
        lax.psum_scatter(
            grad_fc1.astype(jnp.bfloat16), "dp", scatter_dimension=0, tiled=True
        ).astype(jnp.float32),
        lax.psum_scatter(
            grad_fc1_bias.astype(jnp.bfloat16), "dp", scatter_dimension=0, tiled=True
        ).astype(jnp.float32),
        lax.psum_scatter(
            grad_fc2.astype(jnp.bfloat16), "dp", scatter_dimension=1, tiled=True
        ).astype(jnp.float32),
        lax.psum_scatter(
            grad_gain_two.astype(jnp.bfloat16), "dp", scatter_dimension=0, tiled=True
        ).astype(jnp.float32),
        lax.psum_scatter(
            grad_shift_two.astype(jnp.bfloat16), "dp", scatter_dimension=0, tiled=True
        ).astype(jnp.float32),
        lax.psum_scatter(
            grad_fc2_bias.astype(jnp.bfloat16), "dp", scatter_dimension=0, tiled=True
        ).astype(jnp.float32),
    )
    sum_gain_one, sum_shift_one, sum_proj_bias, sum_gain_two, sum_shift_two, sum_fc2_bias = (
        lax.psum(
            (sum_gain_one, sum_shift_one, sum_proj_bias, sum_gain_two, sum_shift_two, sum_fc2_bias),
            "tensor",
        )
    )
    return (
        outputs,
        grad_inputs,
        sum_gain_one,
        sum_shift_one,
        out_qkv,
        out_proj,
        sum_proj_bias,
        sum_gain_two,
        sum_shift_two,
        out_fc1,
        out_fc1_bias,
        out_fc2,
        sum_fc2_bias,
    )


def solution(mesh):
    in_specs = (
        P(("dp", "tensor"), None),
        P(("dp", "tensor"), None),
        P("dp"),
        P(("dp", "tensor")),
        P("dp"),
        P("dp"),
        P(None, "dp", "tensor"),
        P("tensor", "dp"),
        P("dp"),
        P("dp"),
        P("dp"),
        P("dp", "tensor"),
        P(("tensor", "dp")),
        P("tensor", "dp"),
        P("dp"),
    )
    out_specs = (
        P(("dp", "tensor"), None),
        P(("dp", "tensor"), None),
        P("dp"),
        P("dp"),
        P(None, "dp", "tensor"),
        P("tensor", "dp"),
        P("dp"),
        P("dp"),
        P("dp"),
        P("dp", "tensor"),
        P(("tensor", "dp")),
        P("tensor", "dp"),
        P("dp"),
    )
    return jax.shard_map(
        on_device, mesh=mesh, in_specs=in_specs, out_specs=out_specs, check_vma=False
    )
```

profile of v0, /device:TPU:0, one launch (start us, length us, event | category | flops | bytes accessed | tf_op | source)
XLA Modules:
  0.0 1062.3 jit_solution(11267200392812141874)
XLA Ops:
  13.4 78.6 %all-reduce.17 = (bf16[1024]{0:T(1024)(128)(2,1)S(1)}, bf16[1024]{0:T(1024)(128)(2,1)S(1)}, bf16[1024]{0:T(1024)(128)(2,1)S(1)}, bf16[1024]{0:T(1024)(128)(2,1)S(1)}, bf16[1024]{0:T(1024)(128)(2,1)S(1)}) all-reduce(bf16[1024]{0:T(1024)(128)(2,1)S(1)} %dynamic-update-slice.5, ...), channel_id=1, replica_groups=mesh['dp'=16,'tensor'=2] {'dp'}, use_global_device_ids=true, to_apply=%add.5 | all-reduce | flops 5120 | bytes 20480
  104.8 71.6 %all-gather.12.cloned.1.call-done = bf16[3,1024,512]{2,1,0:T(8,128)(2,1)} async-done(((bf16[3,64,512]{2,1,0:T(8,128)(2,1)}), bf16[3,1024,512]{2,1,0:T(8,128)(2,1)}) %all-gather.12.cloned.1.call-update) | async-done | bytes 3145744 | tf_op jit(solution)/shard_map/all_gather | solution.py:121
  176.4 6.2 fusion.13
  190.0 15.7 %fusion.55 = (f32[8,1104]{1,0:T(8,128)S(1)}, f32[8,1104,1104]{1,2,0:T(8,128)}) fusion(bf16[1104,8,64]{0,2,1:T(8,128)(2,1)S(1)} %bitcast.65, bf16[1104,8,64]{0,2,1:T(8,128)(2,1)S(1)} %bitcast.67, pred[1104]{0:T(1024)(128)(4,1)S(1)} %broadcast_compare_fusion), kind=kOutput, calls=%fused_computation.120 | convolution fusion | flops 1277310336 | bytes 41299536 | tf_op jit(solution)/shard_map/while/body/eval_jaxpr/qhd,khd->hqk/dot_general | solution.py:23
  205.7 16.2 %fusion.1 = f32[8,1104]{1,0:T(8,128)S(1)} fusion(f32[8,1104,1104]{1,2,0:T(8,128)} %get-tuple-element.131, f32[8,1104]{1,0:T(8,128)S(1)} %get-tuple-element.130), kind=kLoop, calls=%fused_computation.7 | loop fusion | flops 19492224 | bytes 39072768 | tf_op jit(solution)/shard_map/while/body/eval_jaxpr/reduce_sum | solution.py:32
  221.9 15.8 %fusion.23 = bf16[8,64,1104]{2,1,0:T(8,128)(2,1)S(1)} fusion(bf16[1104,8,64]{0,2,1:T(8,128)(2,1)S(1)} %bitcast.69, f32[8,1104,1104]{1,2,0:T(8,128)} %get-tuple-element.131, f32[8,1104]{1,0:T(8,128)S(1)} %fusion.1, f32[8,1104]{1,0:T(8,128)S(1)} %get-tuple-element.130), kind=kOutput, calls=%fused_computation.55 | convolution fusion | flops 1277884416 | bytes 41333760 | tf_op jit(solution)/shard_map/while/body/eval_jaxpr/hqk,khd->qhd/dot_general | solution.py:34
  244.2 7.2 reduce-scatter.8.cloned.1.call-done
  258.7 40.7 %all-gather = bf16[16,1,128]{2,1,0:T(2,128)(2,1)S(1)} all-gather(bf16[1,1,128]{2,1,0:T(2,128)(2,1)S(1)} %bitcast.75), channel_id=1, replica_groups=mesh['dp'=16,'tensor'=2] {'dp'}, dimensions={0}, use_global_device_ids=true | all-gather | bytes 4352 | tf_op jit(solution)/shard_map/all_gather | solution.py:127
  299.4 31.8 %all-gather.18.cloned.1.call-done = bf16[1024,2048]{1,0:T(8,128)(2,1)} async-done(((bf16[64,2048]{1,0:T(8,128)(2,1)}), bf16[1024,2048]{1,0:T(8,128)(2,1)}) %all-gather.18.cloned.1.call-update) | async-done | bytes 4194320 | tf_op jit(solution)/shard_map/all_gather | solution.py:126
  331.2 11.4 %all-gather.16.cloned.1.call-done = bf16[1104,1024]{1,0:T(8,128)(2,1)} async-done(((bf16[552,1024]{1,0:T(8,128)(2,1)}), bf16[1104,1024]{1,0:T(8,128)(2,1)}) %all-gather.16.cloned.1.call-update) | async-done | bytes 2261008 | tf_op jit(solution)/shard_map/all_gather | solution.py:164
  342.6 11.6 %convolution_add_fusion = f32[1104,2048]{1,0:T(8,128)} fusion(bf16[1104,1024]{1,0:T(8,128)(2,1)} %all-gather.16.cloned.1.call-done, bf16[1024,2048]{1,0:T(8,128)(2,1)} %all-gather.18.cloned.1.call-done, f32[2048]{0:T(1024)S(1)} %bitcast.74), kind=kOutput, calls=%fused_computation.13 | convolution fusion | flops 4632772608 | bytes 15507456 | tf_op jit(solution)/shard_map/dot_general | solution.py:165
  356.8 80.1 %all-gather.20.cloned.1.call-done = bf16[2048,1024]{0,1:T(8,128)(2,1)} async-done(((bf16[2048,64]{0,1:T(8,128)(2,1)}), bf16[2048,1024]{0,1:T(8,128)(2,1)}) %all-gather.20.cloned.1.call-update) | async-done | bytes 4194320 | tf_op jit(solution)/shard_map/all_gather | solution.py:128
  436.8 29.1 %fusion.47 = (bf16[2048]{0:T(1024)(128)(2,1)}, bf16[1104,2048]{1,0:T(8,128)(2,1)S(1)}, f32[1104,2048]{1,0:T(8,128)}) fusion(f32[1104,2048]{1,0:T(8,128)} %convolution_add_fusion, bf16[1104,1024]{1,0:T(8,128)(2,1)} %all-gather.22.cloned.1.call-done, bf16[2048,1024]{0,1:T(8,128)(2,1)} %all-gather.20.cloned.1.call-done), kind=kOutput, calls=%fused_computation.114 | convolution fusion | flops 4795561984 | bytes 29069312 | tf_op jit(solution)/shard_map/dot_general | solution.py:72
  468.1 6.2 convolution_convert_fusion.4
  474.5 8.3 reduce-scatter.12.cloned.1.call-done
  489.8 10.7 %multiply_convert_fusion.1 = bf16[1104,2048]{1,0:T(8,128)(2,1)} fusion(f32[1104,2048]{1,0:T(8,128)} %get-tuple-element.116, f32[1104,2048]{1,0:T(8,128)} %convolution_add_fusion), kind=kLoop, calls=%fused_computation.16 | loop fusion | flops 6782976 | bytes 22609920 | tf_op jit(solution)/shard_map/convert_element_type | solution.py:166
  500.5 9.5 convolution_convert_fusion.2
  511.7 9.5 convolution_convert_fusion.3
  526.1 16.6 %fusion.20 = bf16[8,64,1104]{2,1,0:T(8,128)(2,1)} fusion(bf16[1104,8,64]{0,2,1:T(8,128)(2,1)S(1)} %bitcast.63, f32[8,1104,1104]{1,2,0:T(8,128)} %get-tuple-element.131, f32[8,1104]{1,0:T(8,128)S(1)} %log_add_fusion), kind=kOutput, calls=%fused_computation.53 | convolution fusion | flops 1268133888 | bytes 41298432 | tf_op jit(solution)/shard_map/while/body/eval_jaxpr/hqk,qhd->khd/dot_general | solution.py:52
  542.7 30.0 %multiply_reduce_fusion = (f32[8,1104]{1,0:T(8,128)S(1)}, f32[8,1104,1104]{1,2,0:T(8,128)}) fusion(f32[8,1104,1104]{1,2,0:T(8,128)} %get-tuple-element.131, f32[8,1104]{1,0:T(8,128)S(1)} %log_add_fusion, bf16[1104,8,64]{0,2,1:T(8,128)(2,1)S(1)} %bitcast.64, bf16[1104,8,64]{0,2,1:T(8,128)(2,1)S(1)} %bitcast.70), kind=kOutput, calls=%fused_computation.3 | convolution fusion | flops 1277310336 | bytes 80335872 | tf_op jit(solution)/shard_map/while/body/eval_jaxpr/qhd,khd->hqk/dot_general | solution.py:41
  575.0 33.6 %multiply_convert_fusion = bf16[8,1104,1104]{1,2,0:T(8,128)(2,1)} fusion(f32[8,1104,1104]{1,2,0:T(8,128)} %get-tuple-element.133, f32[8,1104,1104]{1,2,0:T(8,128)} %get-tuple-element.131, f32[8,1104]{1,0:T(8,128)S(1)} %get-tuple-element.132, f32[8,1104]{1,0:T(8,128)S(1)} %log_add_fusion), kind=kLoop, calls=%fused_computation.2 | loop fusion | flops 39002112 | bytes 97575936 | tf_op jit(solution)/shard_map/while/body/eval_jaxpr/convert_element_type | solution.py:43
  608.6 10.4 fusion.18
  625.6 10.3 fusion.19
  637.9 8.0 convert_bitcast_fusion
  645.9 7.6 copy.67
  654.8 6.8 bitcast_convert_fusion
  661.9 9.8 convolution_convert_fusion.5
  675.5 27.9 %reduce-scatter.18.cloned.1.call-done = bf16[64,2048]{1,0:T(8,128)(2,1)} async-done(((bf16[1024,2048]{1,0:T(8,128)(2,1)}), bf16[64,2048]{1,0:T(8,128)(2,1)}) %reduce-scatter.18.cloned.1.call-update) | async-done | bytes 262160 | tf_op jit(solution)/shard_map/reduce_scatter | solution.py:261
  705.2 77.7 %reduce-scatter.16.cloned.1.call-done = bf16[512,64]{0,1:T(8,128)(2,1)} async-done(((bf16[512,1024]{0,1:T(8,128)(2,1)}), bf16[512,64]{0,1:T(8,128)(2,1)}) %reduce-scatter.16.cloned.1.call-update) | async-done | bytes 65552 | tf_op jit(solution)/shard_map/reduce_scatter | solution.py:249
  784.4 169.8 %all-reduce.20.cloned.1.call-done = bf16[3,1024,512]{2,0,1:T(4,128)(2,1)} async-done(((bf16[3,1024,512]{2,0,1:T(4,128)(2,1)}), bf16[3,1024,512]{2,0,1:T(4,128)(2,1)}) %all-reduce.20.cloned.1.call-update) | async-done | bytes 3145744
  956.1 9.0 reduce-scatter.14.cloned.1.call-done
  970.1 77.0 %all-reduce.16 = (bf16[1024]{0:T(1024)(128)(2,1)S(1)}, bf16[1024]{0:T(1024)(128)(2,1)S(1)}, bf16[1024]{0:T(1024)(128)(2,1)S(1)}, bf16[1024]{0:T(1024)(128)(2,1)S...) all-reduce(bf16[1024]{0:T(1024)(128)(2,1)S(1)} %dynamic-update-slic, ...), channel_id=1, replica_groups=mesh['dp'=16,'tensor'=2] {'dp'}, use_global_device_ids=true, to_apply=%add.6 | all-reduce | flops 9216 | bytes 36864
  (202 shorter events, 89.3 us)
Async XLA Ops:
  7.2 89.3 %copy-start = (bf16[552,1024]{1,0:T(8,128)(2,1)S(1)}, bf16[552,1024]{1,0:T(8,128)(2,1)}, u32[]{:S(2)}) copy-start(bf16[552,1024]{1,0:T(8,128)(2,1)} %param.15) | copy-start | bytes 3391492
  7.2 97.6 %all-gather.10.cloned.1.call-start = ((), (), s32[]{:S(2)}) async-start(), calls=%async_computation.7 | async-start | bytes 3391488 | tf_op jit(solution)/shard_map/all_gather | solution.py:138
  98.0 78.4 %all-gather.12.cloned.1.call-start = ((), (), s32[]{:S(2)}) async-start(), calls=%async_computation.8 | async-start | bytes 3342336 | tf_op jit(solution)/shard_map/all_gather | solution.py:121
  98.7 139.1 %all-gather.14.cloned.1.call-start = ((), (), s32[]{:S(2)}) async-start(), calls=%async_computation.9 | async-start | bytes 1114112 | tf_op jit(solution)/shard_map/all_gather | solution.py:122
  99.4 152.0 %reduce-scatter.8.cloned.1.call-start = ((), (), s32[]{:S(2)}) async-start(), calls=%async_computation.10 | async-start | bytes 3391488 | tf_op jit(solution)/shard_map/reduce_scatter | solution.py:153
  187.1 18.6 %copy-start.6 = (bf16[1,1104,512]{1,2,0:T(8,128)(2,1)}, bf16[1,1104,512]{1,2,0:T(8,128)(2,1)S(1)}, u32[]{:S(2)}) copy-start(bf16[1,1104,512]{1,2,0:T(8,128)(2,1)S(1)} %copy.57) | copy-start | bytes 3391492
  205.7 16.2 %copy-start.13 = (bf16[1,1104,512]{1,2,0:T(8,128)(2,1)S(1)}, bf16[1,1104,512]{1,2,0:T(8,128)(2,1)}, u32[]{:S(2)}) copy-start(bf16[1,1104,512]{1,2,0:T(8,128)(2,1)} %copy.56) | copy-start | bytes 3391492
  242.3 88.9 %all-gather.18.cloned.1.call-start = ((), (), s32[]{:S(2)}) async-start(), calls=%async_computation.12 | async-start | bytes 4456448 | tf_op jit(solution)/shard_map/all_gather | solution.py:126
  242.9 99.8 %all-gather.16.cloned.1.call-start = ((), (), s32[]{:S(2)}) async-start(), calls=%async_computation.11 | async-start | bytes 3391488 | tf_op jit(solution)/shard_map/all_gather | solution.py:164
  244.1 242.0 %copy-start.20 = (f32[1024]{0:T(1024)}, f32[1024]{0:T(1024)S(1)}, u32[]{:S(2)}) copy-start(f32[1024]{0:T(1024)S(1)} %convert_element_type.206) | copy-start | bytes 12292
  244.2 243.2 %copy-start.18 = (f32[552]{0:T(1024)}, f32[552]{0:T(1024)S(1)}, u32[]{:S(2)}) copy-start(f32[552]{0:T(1024)S(1)} %fusion.40) | copy-start | bytes 6628
  255.9 100.9 %all-gather.22.cloned.1.call-start = ((), (), s32[]{:S(2)}) async-start(), calls=%async_computation.15 | async-start | bytes 3391488 | tf_op jit(solution)/shard_map/all_gather | solution.py:179
  257.9 178.9 %all-gather.20.cloned.1.call-start = ((), (), s32[]{:S(2)}) async-start(), calls=%async_computation.13 | async-start | bytes 4456448 | tf_op jit(solution)/shard_map/all_gather | solution.py:128
  258.7 224.2 %reduce-scatter.12.cloned.1.call-start = ((), (), s32[]{:S(2)}) async-start(), calls=%async_computation.16 | async-start | bytes 3391488 | tf_op jit(solution)/shard_map/reduce_scatter | solution.py:190
  436.8 31.2 %copy-start.38 = (bf16[1024,2048]{1,0:T(8,128)(2,1)S(1)}, bf16[1024,2048]{1,0:T(8,128)(2,1)}, u32[]{:S(2)}) copy-start(bf16[1024,2048]{1,0:T(8,128)(2,1)} %all-gather.18.cloned.1.call-done) | copy-start | bytes 12582916
  474.3 47.2 %all-gather.24.cloned.1.call-start = ((), (), s32[]{:S(2)}) async-start(), calls=%async_computation.17 | async-start | bytes 3391488 | tf_op jit(solution)/shard_map/all_gather | solution.py:201
  489.8 183.9 %reduce-scatter.20.cloned.1.call-start = ((), (), s32[]{:S(2)}) async-start(), calls=%async_computation.21 | async-start | bytes 4456448 | tf_op jit(solution)/shard_map/reduce_scatter | solution.py:267
  510.1 193.3 %reduce-scatter.18.cloned.1.call-start = ((), (), s32[]{:S(2)}) async-start(), calls=%async_computation.20 | async-start | bytes 4456448 | tf_op jit(solution)/shard_map/reduce_scatter | solution.py:261
  521.2 261.7 %reduce-scatter.16.cloned.1.call-start = ((), (), s32[]{:S(2)}) async-start(), calls=%async_computation.19 | async-start | bytes 1114112 | tf_op jit(solution)/shard_map/reduce_scatter | solution.py:249
  526.1 16.6 %copy-start.14 = (bf16[1,1104,512]{1,2,0:T(8,128)(2,1)S(1)}, bf16[1,1104,512]{1,2,0:T(8,128)(2,1)}, u32[]{:S(2)}) copy-start(bf16[1,1104,512]{1,2,0:T(8,128)(2,1)} %copy.56) | copy-start | bytes 3391492
  575.0 33.6 %copy-start.9 = (bf16[1,1104,512]{1,2,0:T(8,128)(2,1)S(1)}, bf16[1,1104,512]{1,2,0:T(8,128)(2,1)}, u32[]{:S(2)}) copy-start(bf16[1,1104,512]{1,2,0:T(8,128)(2,1)} %copy-done.8) | copy-start | bytes 3391492
  625.1 329.2 %all-reduce.20.cloned.1.call-start = ((), (), s32[]{:S(2)}) async-start(), calls=%async_computation.22 | async-start | bytes 8388608
  653.5 311.6 %reduce-scatter.14.cloned.1.call-start = ((), (), s32[]{:S(2)}) async-start(), calls=%async_computation.18 | async-start | bytes 3391488 | tf_op jit(solution)/shard_map/reduce_scatter | solution.py:222
  661.6 389.3 %reduce-scatter.10.cloned.1.call-start = ((), (), s32[]{:S(2)}) async-start(), calls=%async_computation.14 | async-start | bytes 3391488 | tf_op jit(solution)/shard_map/reduce_scatter | solution.py:168
  673.6 293.1 %copy-start.1 = (bf16[552,1024]{1,0:T(8,128)(2,1)S(1)}, bf16[552,1024]{1,0:T(8,128)(2,1)}, u32[]{:S(2)}) copy-start(bf16[552,1024]{1,0:T(8,128)(2,1)} %param.15) | copy-start | bytes 3391492
  673.6 293.1 %copy-start.23 = (f32[552]{0:T(1024)S(1)}, f32[552]{0:T(1024)}, u32[]{:S(2)}) copy-start(f32[552]{0:T(1024)} %copy-done.22) | copy-start | bytes 6628
  673.6 293.1 %copy-start.25 = (f32[1024]{0:T(1024)S(1)}, f32[1024]{0:T(1024)}, u32[]{:S(2)}) copy-start(f32[1024]{0:T(1024)} %copy-done.24) | copy-start | bytes 12292
  955.3 13.5 %copy-start.27 = (f32[552]{0:T(1024)S(1)}, f32[552]{0:T(1024)}, u32[]{:S(2)}) copy-start(f32[552]{0:T(1024)} %copy-done.26) | copy-start | bytes 6628
  966.8 84.1 %copy-start.3 = (bf16[552,1024]{1,0:T(8,128)(2,1)S(1)}, bf16[552,1024]{1,0:T(8,128)(2,1)}, u32[]{:S(2)}) copy-start(bf16[552,1024]{1,0:T(8,128)(2,1)} %reduce-scatter.8.cloned.1.call-done) | copy-start | bytes 3391492
  966.8 84.1 %copy-start.19 = (f32[552]{0:T(1024)S(1)}, f32[552]{0:T(1024)}, u32[]{:S(2)}) copy-start(f32[552]{0:T(1024)} %copy-done.18) | copy-start | bytes 6628
  966.8 84.1 %copy-start.21 = (f32[1024]{0:T(1024)S(1)}, f32[1024]{0:T(1024)}, u32[]{:S(2)}) copy-start(f32[1024]{0:T(1024)} %copy-done.20) | copy-start | bytes 12292
  966.8 84.1 %copy-start.31 = (f32[552]{0:T(1024)S(1)}, f32[552]{0:T(1024)}, u32[]{:S(2)}) copy-start(f32[552]{0:T(1024)} %copy-done.30) | copy-start | bytes 6628
  (30 other events, 103.1 us)
Sparse Core Ops, SparseCore 0:
  98.1 6.6 all-gather.9
  107.6 68.7 all-gather.11
  179.1 54.3 all-gather.13
  242.4 8.9 reduce-scatter.7
  254.0 77.1 all-gather.17
  333.2 9.4 all-gather.15
  344.8 11.9 all-gather.21
  359.6 77.2 all-gather.19
  474.4 8.3 reduce-scatter.11
  489.9 11.9 all-gather.23
  510.2 96.2 reduce-scatter.19
  608.6 94.7 reduce-scatter.17
  705.7 77.2 reduce-scatter.15
  789.3 164.8 all-reduce.19
  956.4 8.7 reduce-scatter.13
  967.3 10.9 reduce-scatter.9
where the time goes:
time: 1070 us; the launch traced here: 1060 us
  waiting for transfers between devices  501 us (47%)
  matrix products  208 us (19%)
  blocking collectives  202 us (19%)
  other arithmetic  95 us (9%)
  local copies, waits for them, and re-layouts  36 us (3%)
  between operations  18.1 us (2%)
    unnamed x17, waiting for transfers between devices  173 us
    unnamed x3, blocking collectives  158 us
    all_gather x1, waiting for transfers between devices, on_device(): lax.all_gather(fc2_weight, 'dp', axis=1, tiled=True)  80.1 us
    reduce_scatter x1, waiting for transfers between devices, on_device(): lax.psum_scatter(grad_proj.astype(jnp.bfloat16), 'dp', scatter_dimension=...  77.7 us
    all_gather x1, waiting for transfers between devices, on_device(): lax.all_gather(qkv_weight, 'dp', axis=1, tiled=True)  71.6 us
    all_gather x1, blocking collectives, on_device(): lax.all_gather(fc1_bias, 'dp', axis=0, tiled=True)  40.7 us
    dot_general x3, matrix products, contract_cols(): lax.dot_general(left, right, (((1,), (1,)), ((), ())), preferred_element_...  38.3 us
    convert_element_type x1, other arithmetic, attend_backward(): grad_scores = (attn_prob * (grad_prob - row_dot)).astype(jnp.bfloat16)  33.6 us
  transfers between devices with their start and end apart: 16, of which 12 were waited for; matrix products, arithmetic and copies ran while one was open for 25% of the time, Pallas kernels for 0%

commit v1 on v0

--- a/solution.py
+++ b/solution.py
@@ -1,3 +1,4 @@
+import functools
 import jax
 import jax.numpy as jnp
 from jax import lax
@@ -5,6 +6,18 @@
 
 HEAD_DIM = 64
 SEQ_LEN = 1104
+
+
+def views_convert(mat, lane_axis):
+    windows = []
+    for _ in range(lax.axis_size(lane_axis)):
+        windows.append(mat)
+    return jnp.concatenate(
+        lax.all_to_all(jnp.stack(windows), split_axis=0, concat_axis=0, axis_name=lane_axis), axis=0
+    )
+
+
+scan_knots_all = functools.partial(views_convert, lane_axis="dp")
 
 
 def layer_norm(values, norm_gain, norm_shift):
@@ -124,7 +137,7 @@
         lax.all_gather(attn_norm_gain, "dp", axis=0, tiled=True),
         lax.all_gather(attn_norm_bias, "dp", axis=0, tiled=True),
         lax.all_gather(fc1_weight, "dp", axis=0, tiled=True),
-        lax.all_gather(fc1_bias, "dp", axis=0, tiled=True),
+        scan_knots_all(fc1_bias),
         lax.all_gather(fc2_weight, "dp", axis=1, tiled=True),
         lax.all_gather(mlp_norm_gain, "dp", axis=0, tiled=True),
         lax.all_gather(mlp_norm_bias, "dp", axis=0, tiled=True),

time: 1070 us -> 1070 us (level)
  blocking collectives: 202 us -> 175 us
  waiting for transfers between devices: 501 us -> 528 us
    all_gather x1 -> x0, blocking collectives: 40.7 us -> none  [on_device(): lax.all_gather(fc1_bias, 'dp', axis=0, tiled=True)]
    all_gather x1, waiting for transfers between devices: 31.8 us -> 58.8 us  [on_device(): lax.all_gather(fc1_weight, 'dp', axis=0, tiled=True)]
    all_to_all x0 -> x1, blocking collectives: none -> 13.8 us  [views_convert(): lax.all_to_all(jnp.stack(windows), split_axis=0, concat_axis=0, axis_name...]
where the time goes in v1:
time: 1070 us; the launch traced here: 1060 us
  waiting for transfers between devices  528 us (49%)
  matrix products  208 us (19%)
  blocking collectives  175 us (16%)
  other arithmetic  95 us (9%)
  local copies, waits for them, and re-layouts  36 us (3%)
  between operations  18.2 us (2%)
    unnamed x17, waiting for transfers between devices  173 us
    unnamed x3, blocking collectives  158 us
    all_gather x1, waiting for transfers between devices, on_device(): lax.all_gather(fc2_weight, 'dp', axis=1, tiled=True)  80.1 us
    reduce_scatter x1, waiting for transfers between devices, on_device(): lax.psum_scatter(grad_proj.astype(jnp.bfloat16), 'dp', scatter_dimension=...  77.7 us
    all_gather x1, waiting for transfers between devices, on_device(): lax.all_gather(qkv_weight, 'dp', axis=1, tiled=True)  71.6 us
    all_gather x1, waiting for transfers between devices, on_device(): lax.all_gather(fc1_weight, 'dp', axis=0, tiled=True)  58.8 us
    dot_general x3, matrix products, contract_cols(): lax.dot_general(left, right, (((1,), (1,)), ((), ())), preferred_element_...  38.3 us
    convert_element_type x1, other arithmetic, attend_backward(): grad_scores = (attn_prob * (grad_prob - row_dot)).astype(jnp.bfloat16)  33.6 us
  transfers between devices with their start and end apart: 16, of which 12 were waited for; matrix products, arithmetic and copies ran while one was open for 25% of the time, Pallas kernels for 0%

profile of v1, /device:TPU:0, one launch (start us, length us, event | category | flops | bytes accessed | tf_op | source)
XLA Modules:
  0.0 1062.4 jit_solution(2529646889940063638)
XLA Ops:
  13.4 78.6 %all-reduce.17 = (bf16[1024]{0:T(1024)(128)(2,1)S(1)}, bf16[1024]{0:T(1024)(128)(2,1)S(1)}, bf16[1024]{0:T(1024)(128)(2,1)S(1)}, bf16[1024]{0:T(1024)(128)(2,1)S(1)}, bf16[1024]{0:T(1024)(128)(2,1)S(1)}) all-reduce(bf16[1024]{0:T(1024)(128)(2,1)S(1)} %dynamic-update-slice.5, ...), channel_id=1, replica_groups=mesh['dp'=16,'tensor'=2] {'dp'}, use_global_device_ids=true, to_apply=%add.5 | all-reduce | flops 5120 | bytes 20480
  104.8 71.6 %all-gather.11.cloned.1.call-done = bf16[3,1024,512]{2,1,0:T(8,128)(2,1)} async-done(((bf16[3,64,512]{2,1,0:T(8,128)(2,1)}), bf16[3,1024,512]{2,1,0:T(8,128)(2,1)}) %all-gather.11.cloned.1.call-update) | async-done | bytes 3145744 | tf_op jit(solution)/shard_map/all_gather | solution.py:134
  176.4 6.2 fusion.13
  190.0 15.7 %fusion.55 = (f32[8,1104]{1,0:T(8,128)S(1)}, f32[8,1104,1104]{1,2,0:T(8,128)}) fusion(bf16[1104,8,64]{0,2,1:T(8,128)(2,1)S(1)} %bitcast.64, bf16[1104,8,64]{0,2,1:T(8,128)(2,1)S(1)} %bitcast.66, pred[1104]{0:T(1024)(128)(4,1)S(1)} %broadcast_compare_fusion), kind=kOutput, calls=%fused_computation.120 | convolution fusion | flops 1277310336 | bytes 41299536 | tf_op jit(solution)/shard_map/while/body/eval_jaxpr/qhd,khd->hqk/dot_general | solution.py:36
  205.7 16.2 %fusion.1 = f32[8,1104]{1,0:T(8,128)S(1)} fusion(f32[8,1104,1104]{1,2,0:T(8,128)} %get-tuple-element.131, f32[8,1104]{1,0:T(8,128)S(1)} %get-tuple-element.130), kind=kLoop, calls=%fused_computation.7 | loop fusion | flops 19492224 | bytes 39072768 | tf_op jit(solution)/shard_map/while/body/eval_jaxpr/reduce_sum | solution.py:45
  221.9 15.8 %fusion.23 = bf16[8,64,1104]{2,1,0:T(8,128)(2,1)S(1)} fusion(bf16[1104,8,64]{0,2,1:T(8,128)(2,1)S(1)} %bitcast.68, f32[8,1104,1104]{1,2,0:T(8,128)} %get-tuple-element.131, f32[8,1104]{1,0:T(8,128)S(1)} %fusion.1, f32[8,1104]{1,0:T(8,128)S(1)} %get-tuple-element.130), kind=kOutput, calls=%fused_computation.55 | convolution fusion | flops 1277884416 | bytes 41333760 | tf_op jit(solution)/shard_map/while/body/eval_jaxpr/hqk,khd->qhd/dot_general | solution.py:47
  244.2 7.2 reduce-scatter.8.cloned.1.call-done
  258.7 13.8 %all_to_all.6 = bf16[16,1,128]{2,1,0:T(2,128)(2,1)S(1)} all-to-all(bf16[16,1,128]{2,1,0:T(2,128)(2,1)S(1)} %stack.10), channel_id=1, replica_groups=mesh['dp'=16,'tensor'=2] {'dp'}, dimensions={0} | all-to-all | bytes 8192 | tf_op jit(solution)/shard_map/all_to_all | solution.py:16
  272.6 58.8 %all-gather.17.cloned.1.call-done = bf16[1024,2048]{1,0:T(8,128)(2,1)} async-done(((bf16[64,2048]{1,0:T(8,128)(2,1)}), bf16[1024,2048]{1,0:T(8,128)(2,1)}) %all-gather.17.cloned.1.call-update) | async-done | bytes 4194320 | tf_op jit(solution)/shard_map/all_gather | solution.py:139
  331.3 11.4 %all-gather.15.cloned.1.call-done = bf16[1104,1024]{1,0:T(8,128)(2,1)} async-done(((bf16[552,1024]{1,0:T(8,128)(2,1)}), bf16[1104,1024]{1,0:T(8,128)(2,1)}) %all-gather.15.cloned.1.call-update) | async-done | bytes 2261008 | tf_op jit(solution)/shard_map/all_gather | solution.py:177
  342.7 11.6 %convolution_add_fusion = f32[1104,2048]{1,0:T(8,128)} fusion(bf16[1104,1024]{1,0:T(8,128)(2,1)} %all-gather.15.cloned.1.call-done, bf16[1024,2048]{1,0:T(8,128)(2,1)} %all-gather.17.cloned.1.call-done, f32[2048]{0:T(1024)S(1)} %bitcast.73), kind=kOutput, calls=%fused_computation.13 | convolution fusion | flops 4632772608 | bytes 15507456 | tf_op jit(solution)/shard_map/dot_general | solution.py:178
  356.9 80.1 %all-gather.19.cloned.1.call-done = bf16[2048,1024]{0,1:T(8,128)(2,1)} async-done(((bf16[2048,64]{0,1:T(8,128)(2,1)}), bf16[2048,1024]{0,1:T(8,128)(2,1)}) %all-gather.19.cloned.1.call-update) | async-done | bytes 4194320 | tf_op jit(solution)/shard_map/all_gather | solution.py:141
  436.9 29.1 %fusion.47 = (bf16[2048]{0:T(1024)(128)(2,1)}, bf16[1104,2048]{1,0:T(8,128)(2,1)S(1)}, f32[1104,2048]{1,0:T(8,128)}) fusion(f32[1104,2048]{1,0:T(8,128)} %convolution_add_fusion, bf16[1104,1024]{1,0:T(8,128)(2,1)} %all-gather.21.cloned.1.call-done, bf16[2048,1024]{0,1:T(8,128)(2,1)} %all-gather.19.cloned.1.call-done), kind=kOutput, calls=%fused_computation.114 | convolution fusion | flops 4795561984 | bytes 29069312 | tf_op jit(solution)/shard_map/dot_general | solution.py:85
  468.2 6.2 convolution_convert_fusion.4
  474.6 8.3 reduce-scatter.12.cloned.1.call-done
  489.9 10.7 %multiply_convert_fusion.1 = bf16[1104,2048]{1,0:T(8,128)(2,1)} fusion(f32[1104,2048]{1,0:T(8,128)} %get-tuple-element.116, f32[1104,2048]{1,0:T(8,128)} %convolution_add_fusion), kind=kLoop, calls=%fused_computation.16 | loop fusion | flops 6782976 | bytes 22609920 | tf_op jit(solution)/shard_map/convert_element_type | solution.py:179
  500.6 9.5 convolution_convert_fusion.2
  511.8 9.5 convolution_convert_fusion.3
  526.2 16.6 %fusion.20 = bf16[8,64,1104]{2,1,0:T(8,128)(2,1)} fusion(bf16[1104,8,64]{0,2,1:T(8,128)(2,1)S(1)} %bitcast.62, f32[8,1104,1104]{1,2,0:T(8,128)} %get-tuple-element.131, f32[8,1104]{1,0:T(8,128)S(1)} %log_add_fusion), kind=kOutput, calls=%fused_computation.53 | convolution fusion | flops 1268133888 | bytes 41298432 | tf_op jit(solution)/shard_map/while/body/eval_jaxpr/hqk,qhd->khd/dot_general | solution.py:65
  542.8 30.0 %multiply_reduce_fusion = (f32[8,1104]{1,0:T(8,128)S(1)}, f32[8,1104,1104]{1,2,0:T(8,128)}) fusion(f32[8,1104,1104]{1,2,0:T(8,128)} %get-tuple-element.131, f32[8,1104]{1,0:T(8,128)S(1)} %log_add_fusion, bf16[1104,8,64]{0,2,1:T(8,128)(2,1)S(1)} %bitcast.63, bf16[1104,8,64]{0,2,1:T(8,128)(2,1)S(1)} %bitcast.69), kind=kOutput, calls=%fused_computation.3 | convolution fusion | flops 1277310336 | bytes 80335872 | tf_op jit(solution)/shard_map/while/body/eval_jaxpr/qhd,khd->hqk/dot_general | solution.py:54
  575.1 33.6 %multiply_convert_fusion = bf16[8,1104,1104]{1,2,0:T(8,128)(2,1)} fusion(f32[8,1104,1104]{1,2,0:T(8,128)} %get-tuple-element.133, f32[8,1104,1104]{1,2,0:T(8,128)} %get-tuple-element.131, f32[8,1104]{1,0:T(8,128)S(1)} %get-tuple-element.132, f32[8,1104]{1,0:T(8,128)S(1)} %log_add_fusion), kind=kLoop, calls=%fused_computation.2 | loop fusion | flops 39002112 | bytes 97575936 | tf_op jit(solution)/shard_map/while/body/eval_jaxpr/convert_element_type | solution.py:56
  608.7 10.4 fusion.18
  625.7 10.3 fusion.19
  638.0 8.0 convert_bitcast_fusion
  646.0 7.6 copy.67
  654.9 6.8 bitcast_convert_fusion
  662.0 9.8 convolution_convert_fusion.5
  675.6 27.9 %reduce-scatter.18.cloned.1.call-done = bf16[64,2048]{1,0:T(8,128)(2,1)} async-done(((bf16[1024,2048]{1,0:T(8,128)(2,1)}), bf16[64,2048]{1,0:T(8,128)(2,1)}) %reduce-scatter.18.cloned.1.call-update) | async-done | bytes 262160 | tf_op jit(solution)/shard_map/reduce_scatter | solution.py:274
  705.3 77.7 %reduce-scatter.16.cloned.1.call-done = bf16[512,64]{0,1:T(8,128)(2,1)} async-done(((bf16[512,1024]{0,1:T(8,128)(2,1)}), bf16[512,64]{0,1:T(8,128)(2,1)}) %reduce-scatter.16.cloned.1.call-update) | async-done | bytes 65552 | tf_op jit(solution)/shard_map/reduce_scatter | solution.py:262
  784.5 169.8 %all-reduce.20.cloned.1.call-done = bf16[3,1024,512]{2,0,1:T(4,128)(2,1)} async-done(((bf16[3,1024,512]{2,0,1:T(4,128)(2,1)}), bf16[3,1024,512]{2,0,1:T(4,128)(2,1)}) %all-reduce.20.cloned.1.call-update) | async-done | bytes 3145744
  956.2 9.0 reduce-scatter.14.cloned.1.call-done
  970.2 77.0 %all-reduce.16 = (bf16[1024]{0:T(1024)(128)(2,1)S(1)}, bf16[1024]{0:T(1024)(128)(2,1)S(1)}, bf16[1024]{0:T(1024)(128)(2,1)S(1)}, bf16[1024]{0:T(1024)(128)(2,1)S...) all-reduce(bf16[1024]{0:T(1024)(128)(2,1)S(1)} %dynamic-update-slic, ...), channel_id=1, replica_groups=mesh['dp'=16,'tensor'=2] {'dp'}, use_global_device_ids=true, to_apply=%add.6 | all-reduce | flops 9216 | bytes 36864
  (203 shorter events, 89.3 us)
Async XLA Ops:
  7.2 89.3 %copy-start = (bf16[552,1024]{1,0:T(8,128)(2,1)S(1)}, bf16[552,1024]{1,0:T(8,128)(2,1)}, u32[]{:S(2)}) copy-start(bf16[552,1024]{1,0:T(8,128)(2,1)} %param.15) | copy-start | bytes 3391492
  7.2 97.6 %all-gather.9.cloned.1.call-start = ((), (), s32[]{:S(2)}) async-start(), calls=%async_computation.8 | async-start | bytes 3391488 | tf_op jit(solution)/shard_map/all_gather | solution.py:151
  98.0 78.4 %all-gather.11.cloned.1.call-start = ((), (), s32[]{:S(2)}) async-start(), calls=%async_computation.9 | async-start | bytes 3342336 | tf_op jit(solution)/shard_map/all_gather | solution.py:134
  98.7 139.1 %all-gather.13.cloned.1.call-start = ((), (), s32[]{:S(2)}) async-start(), calls=%async_computation.10 | async-start | bytes 1114112 | tf_op jit(solution)/shard_map/all_gather | solution.py:135
  99.4 152.0 %reduce-scatter.8.cloned.1.call-start = ((), (), s32[]{:S(2)}) async-start(), calls=%async_computation.11 | async-start | bytes 3391488 | tf_op jit(solution)/shard_map/reduce_scatter | solution.py:166
  187.1 18.6 %copy-start.6 = (bf16[1,1104,512]{1,2,0:T(8,128)(2,1)}, bf16[1,1104,512]{1,2,0:T(8,128)(2,1)S(1)}, u32[]{:S(2)}) copy-start(bf16[1,1104,512]{1,2,0:T(8,128)(2,1)S(1)} %copy.57) | copy-start | bytes 3391492
  205.7 16.2 %copy-start.13 = (bf16[1,1104,512]{1,2,0:T(8,128)(2,1)S(1)}, bf16[1,1104,512]{1,2,0:T(8,128)(2,1)}, u32[]{:S(2)}) copy-start(bf16[1,1104,512]{1,2,0:T(8,128)(2,1)} %copy.56) | copy-start | bytes 3391492
  242.3 89.0 %all-gather.17.cloned.1.call-start = ((), (), s32[]{:S(2)}) async-start(), calls=%async_computation.13 | async-start | bytes 4456448 | tf_op jit(solution)/shard_map/all_gather | solution.py:139
  242.9 99.9 %all-gather.15.cloned.1.call-start = ((), (), s32[]{:S(2)}) async-start(), calls=%async_computation.12 | async-start | bytes 3391488 | tf_op jit(solution)/shard_map/all_gather | solution.py:177
  244.1 242.1 %copy-start.20 = (f32[1024]{0:T(1024)}, f32[1024]{0:T(1024)S(1)}, u32[]{:S(2)}) copy-start(f32[1024]{0:T(1024)S(1)} %convert_element_type.213) | copy-start | bytes 12292
  244.2 243.3 %copy-start.18 = (f32[552]{0:T(1024)}, f32[552]{0:T(1024)S(1)}, u32[]{:S(2)}) copy-start(f32[552]{0:T(1024)S(1)} %fusion.40) | copy-start | bytes 6628
  255.9 101.0 %all-gather.21.cloned.1.call-start = ((), (), s32[]{:S(2)}) async-start(), calls=%async_computation.16 | async-start | bytes 3391488 | tf_op jit(solution)/shard_map/all_gather | solution.py:192
  257.9 179.0 %all-gather.19.cloned.1.call-start = ((), (), s32[]{:S(2)}) async-start(), calls=%async_computation.14 | async-start | bytes 4456448 | tf_op jit(solution)/shard_map/all_gather | solution.py:141
  258.7 224.3 %reduce-scatter.12.cloned.1.call-start = ((), (), s32[]{:S(2)}) async-start(), calls=%async_computation.17 | async-start | bytes 3391488 | tf_op jit(solution)/shard_map/reduce_scatter | solution.py:203
  436.9 31.2 %copy-start.38 = (bf16[1024,2048]{1,0:T(8,128)(2,1)S(1)}, bf16[1024,2048]{1,0:T(8,128)(2,1)}, u32[]{:S(2)}) copy-start(bf16[1024,2048]{1,0:T(8,128)(2,1)} %all-gather.17.cloned.1.call-done) | copy-start | bytes 12582916
  474.4 47.2 %all-gather.23.cloned.1.call-start = ((), (), s32[]{:S(2)}) async-start(), calls=%async_computation.18 | async-start | bytes 3391488 | tf_op jit(solution)/shard_map/all_gather | solution.py:214
  489.9 183.9 %reduce-scatter.20.cloned.1.call-start = ((), (), s32[]{:S(2)}) async-start(), calls=%async_computation.22 | async-start | bytes 4456448 | tf_op jit(solution)/shard_map/reduce_scatter | solution.py:280
  510.2 193.3 %reduce-scatter.18.cloned.1.call-start = ((), (), s32[]{:S(2)}) async-start(), calls=%async_computation.21 | async-start | bytes 4456448 | tf_op jit(solution)/shard_map/reduce_scatter | solution.py:274
  521.3 261.7 %reduce-scatter.16.cloned.1.call-start = ((), (), s32[]{:S(2)}) async-start(), calls=%async_computation.20 | async-start | bytes 1114112 | tf_op jit(solution)/shard_map/reduce_scatter | solution.py:262
  526.2 16.6 %copy-start.14 = (bf16[1,1104,512]{1,2,0:T(8,128)(2,1)S(1)}, bf16[1,1104,512]{1,2,0:T(8,128)(2,1)}, u32[]{:S(2)}) copy-start(bf16[1,1104,512]{1,2,0:T(8,128)(2,1)} %copy.56) | copy-start | bytes 3391492
  575.1 33.6 %copy-start.9 = (bf16[1,1104,512]{1,2,0:T(8,128)(2,1)S(1)}, bf16[1,1104,512]{1,2,0:T(8,128)(2,1)}, u32[]{:S(2)}) copy-start(bf16[1,1104,512]{1,2,0:T(8,128)(2,1)} %copy-done.8) | copy-start | bytes 3391492
  625.2 329.2 %all-reduce.20.cloned.1.call-start = ((), (), s32[]{:S(2)}) async-start(), calls=%async_computation.23 | async-start | bytes 8388608
  653.6 311.6 %reduce-scatter.14.cloned.1.call-start = ((), (), s32[]{:S(2)}) async-start(), calls=%async_computation.19 | async-start | bytes 3391488 | tf_op jit(solution)/shard_map/reduce_scatter | solution.py:235
  661.7 389.3 %reduce-scatter.10.cloned.1.call-start = ((), (), s32[]{:S(2)}) async-start(), calls=%async_computation.15 | async-start | bytes 3391488 | tf_op jit(solution)/shard_map/reduce_scatter | solution.py:181
  673.7 293.1 %copy-start.1 = (bf16[552,1024]{1,0:T(8,128)(2,1)S(1)}, bf16[552,1024]{1,0:T(8,128)(2,1)}, u32[]{:S(2)}) copy-start(bf16[552,1024]{1,0:T(8,128)(2,1)} %param.15) | copy-start | bytes 3391492
  673.7 293.1 %copy-start.23 = (f32[552]{0:T(1024)S(1)}, f32[552]{0:T(1024)}, u32[]{:S(2)}) copy-start(f32[552]{0:T(1024)} %copy-done.22) | copy-start | bytes 6628
  673.7 293.1 %copy-start.25 = (f32[1024]{0:T(1024)S(1)}, f32[1024]{0:T(1024)}, u32[]{:S(2)}) copy-start(f32[1024]{0:T(1024)} %copy-done.24) | copy-start | bytes 12292
  955.4 13.5 %copy-start.27 = (f32[552]{0:T(1024)S(1)}, f32[552]{0:T(1024)}, u32[]{:S(2)}) copy-start(f32[552]{0:T(1024)} %copy-done.26) | copy-start | bytes 6628
  966.9 84.1 %copy-start.3 = (bf16[552,1024]{1,0:T(8,128)(2,1)S(1)}, bf16[552,1024]{1,0:T(8,128)(2,1)}, u32[]{:S(2)}) copy-start(bf16[552,1024]{1,0:T(8,128)(2,1)} %reduce-scatter.8.cloned.1.call-done) | copy-start | bytes 3391492
  966.9 84.1 %copy-start.19 = (f32[552]{0:T(1024)S(1)}, f32[552]{0:T(1024)}, u32[]{:S(2)}) copy-start(f32[552]{0:T(1024)} %copy-done.18) | copy-start | bytes 6628
  966.9 84.1 %copy-start.21 = (f32[1024]{0:T(1024)S(1)}, f32[1024]{0:T(1024)}, u32[]{:S(2)}) copy-start(f32[1024]{0:T(1024)} %copy-done.20) | copy-start | bytes 12292
  966.9 84.1 %copy-start.31 = (f32[552]{0:T(1024)S(1)}, f32[552]{0:T(1024)}, u32[]{:S(2)}) copy-start(f32[552]{0:T(1024)} %copy-done.30) | copy-start | bytes 6628
  (30 other events, 103.1 us)
Sparse Core Ops, SparseCore 0:
  98.1 6.6 all-gather.8
  107.6 68.7 all-gather.10
  179.1 54.3 all-gather.12
  242.4 8.9 reduce-scatter.7
  254.0 77.2 all-gather.16
  333.3 9.4 all-gather.14
  344.9 11.9 all-gather.20
  359.7 77.2 all-gather.18
  474.5 8.3 reduce-scatter.11
  490.0 11.9 all-gather.22
  510.3 96.2 reduce-scatter.19
  608.7 94.7 reduce-scatter.17
  705.8 77.2 reduce-scatter.15
  789.5 164.8 all-reduce.19
  956.5 8.7 reduce-scatter.13
  967.4 10.9 reduce-scatter.9
